TPU v7x, 256 devices: a whole 4x4x8 slice. The times are simulated.
256 devices in a mesh: dp: 32 (over x, z_lo, core), expert: 8 (over y, z_hi).
Axes of the slice: x: 4, y: 4, z: 8 (z_hi: 2, z_lo: 4; z = z_hi * 4 + z_lo), core: 2. Of those that a mesh axis runs over, the one named last changes fastest.
Arguments:
- grad_out: bfloat16 [131072, 3072], P(('dp', 'expert')), may hold values from -0.19921875 to 0.19921875
- expert_ids: int32 [131072, 2], P(('dp', 'expert')), may hold values from 0 to 7, all different within a row; in each aligned block of 512 rows (0 to 511, 512 to 1023, ...) at most 192 rows name the same one
- gate_probs: float32 [131072, 2], P(('dp', 'expert')), may hold values from 0.1 to 1
- saved_gate: bfloat16 [49152, 8, 1024], P('dp', 'expert'), may hold values from -6 to 6
- saved_up: bfloat16 [49152, 8, 1024], P('dp', 'expert'), may hold values from -6 to 6
- master: float32 [8, 1024, 3072], P('expert', 'dp')
- moment_one: float32 [8, 1024, 3072], P('expert', 'dp'), may hold values from -2 to 2
- moment_two: float32 [8, 1024, 3072], P('expert', 'dp'), may hold values from 0.05 to 1
Outputs:
- new_master: float32 [8, 1024, 3072], P('expert', 'dp')
- new_moment_one: float32 [8, 1024, 3072], P('expert', 'dp')
- new_moment_two: float32 [8, 1024, 3072], P('expert', 'dp')
- new_weights: float32 [8, 1024, 3072], P('expert')
Inputs may be any that keep to these rules, and one draw needn't show every extreme that they name: `expert_ids`: in each aligned block of 512 rows (the tokens of one device) no expert is named by more than 192 rows, a bound that some block reaches.
All inputs are finite; a program needn't handle non-finite values.
Results may differ from a plain program's by a relative error of at most 0.00035.
Values may be sent and summed in bfloat16 or wider, within the bound.
A program may use at most 128 MiB of HBM per device.

v0:
```python
import jax
import jax.numpy as jnp
from jax import lax
from jax.sharding import PartitionSpec as P


def local(grad_out, expert_ids, gate_probs, saved_gate, saved_up, master, moment_one, moment_two):
    tok_rows = grad_out.shape[0]
    cap_rows = tok_rows * 3 // 8
    hit = expert_ids == 0
    chosen = jnp.any(hit, axis=1)
    weight = jnp.sum(jnp.where(hit, gate_probs, jnp.float32(0.0)), axis=1)
    slot = jnp.cumsum(chosen.astype(jnp.int32)) - 1
    scaled = (weight[:, None] * grad_out.astype(jnp.float32)).astype(jnp.bfloat16)
    places = jnp.arange(cap_rows, dtype=jnp.int32)
    placing = ((slot[None, :] == places[:, None]) & chosen[None, :]).astype(jnp.bfloat16)
    dispatched = jnp.dot(placing, scaled, preferred_element_type=jnp.float32).astype(jnp.bfloat16)
    slot_rows = saved_gate.shape[0]
    width = saved_gate.shape[2]
    gate_part = saved_gate.reshape(slot_rows, width)
    up_part = saved_up.reshape(slot_rows, width)
    hidden = (jax.nn.silu(gate_part.astype(jnp.float32)) * up_part.astype(jnp.float32)).astype(
        jnp.bfloat16
    )
    contract = (((0,), (0,)), ((), ()))
    everyone = lax.all_gather(dispatched, "expert", axis=0, tiled=True)
    total = lax.dot_general(hidden, everyone, contract, preferred_element_type=jnp.float32)
    grad_slice = lax.psum_scatter(total, "dp", scatter_dimension=0, tiled=True)
    grad = grad_slice.reshape(master.shape)
    new_one = 0.9 * moment_one + 0.1 * grad
    new_two = 0.95 * moment_two + 0.05 * grad * grad
    step = new_one / (1.0 - 0.9**20) / (jnp.sqrt(new_two / (1.0 - 0.95**20)) + 1e-08)
    wrms = jnp.sqrt(jnp.mean(master * master, axis=-1, keepdims=True) + 1e-06)
    srms = jnp.sqrt(jnp.mean(step * step, axis=-1, keepdims=True) + 1e-06)
    factor = jnp.minimum(1.0, 0.02 * wrms / (0.01 * srms))
    new_master = master - 0.01 * factor * step
    gathered = lax.all_gather(new_master, "dp", axis=1, tiled=True)
    return (new_master, new_one, new_two, gathered)


def solution(mesh):
    return jax.shard_map(
        local,
        mesh=mesh,
        in_specs=(
            P(("dp", "expert"), None),
            P(("dp", "expert"), None),
            P(("dp", "expert"), None),
            P("dp", "expert", None),
            P("dp", "expert", None),
            P("expert", "dp", None),
            P("expert", "dp", None),
            P("expert", "dp", None),
        ),
        out_specs=(
            P("expert", "dp", None),
            P("expert", "dp", None),
            P("expert", "dp", None),
            P("expert", None, None),
        ),
        check_vma=False,
    )
```

profile of v0, /device:TPU:1, one launch (start us, length us, event | category | flops | bytes accessed | tf_op | source)
XLA Modules:
  0.0 490.4 jit_solution(2230872570642506750)
XLA Ops:
  7.2 0.0 copy-start.5
  7.2 0.0 all-gather.3.cloned.1.call-start
  7.2 0.9 fusion.17
  8.1 0.3 reduce-window.9
  8.4 0.1 slice.7
  8.5 0.1 slice_reduce_fusion
  8.6 0.1 add_bitcast_fusion
  8.7 0.7 select_reduce_fusion
  9.4 3.8 convolution_convert_fusion
  13.2 0.0 all-gather.3.cloned.1.call-update
  13.3 0.0 reduce-scatter.2.cloned.1.call-start
  13.3 193.8 %all-gather.3.cloned.1.call-done = bf16[1536,3072]{1,0:T(8,128)(2,1)} async-done(((bf16[192,3072]{1,0:T(8,128)(2,1)}), bf16[1536,3072]{1,0:T(8,128)(2,1)}) %all-gather.3.cloned.1.call-update) | async-done | bytes 9437200 | tf_op jit(solution)/shard_map/all_gather | solution.py:26
  207.1 0.0 copy-done.5
  207.1 17.5 %fusion.5 = f32[1024,3072]{1,0:T(8,128)} fusion(bf16[1536,3072]{1,0:T(8,128)(2,1)} %all-gather.3.cloned.1.call-done, bf16[1536,1,1024]{2,0,1:T(8,128)(2,1)S(1)} %copy-done.5, bf16[1536,1,1024]{2,0,1:T(8,128)(2,1)} %param.11), kind=kOutput, calls=%fused_computation.9 | convolution fusion | flops 9676259328 | bytes 28311552 | tf_op jit(solution)/shard_map/dot_general | solution.py:27
  224.6 0.0 copy-start
  224.6 0.0 copy-start.3
  224.6 0.0 copy-start.4
  224.6 0.0 reduce-scatter.2.cloned.1.call-update
  224.7 0.0 all-gather.5.cloned.1.call-start
  224.7 0.9 copy-done
  225.6 0.1 multiply_reduce_fusion.1
  225.8 164.9 %reduce-scatter.2.cloned.1.call-done = f32[32,3072]{1,0:T(8,128)} async-done(((f32[1024,3072]{1,0:T(8,128)}), f32[32,3072]{1,0:T(8,128)}) %reduce-scatter.2.cloned.1.call-update) | async-done | bytes 393232 | tf_op jit(solution)/shard_map/reduce_scatter | solution.py:28
  390.7 0.0 copy-done.3
  390.7 0.0 copy-done.4
  390.7 1.4 multiply_reduce_fusion
  392.0 0.0 copy-start.1
  392.1 0.0 copy-start.2
  392.1 1.0 multiply_subtract_fusion
  393.1 0.0 all-gather.5.cloned.1.call-update
  393.1 79.8 %all-gather.5.cloned.1.call-done = f32[1,1024,3072]{2,1,0:T(8,128)} async-done(((f32[1,32,3072]{2,1,0:T(8,128)}), f32[1,1024,3072]{2,1,0:T(8,128)}) %all-gather.5.cloned.1.call-update) | async-done | bytes 12582928 | tf_op jit(solution)/shard_map/all_gather | solution.py:37
  472.9 11.0 %copy.13 = f32[1,1024,3072]{2,1,0:T(8,128)} copy(f32[1,1024,3072]{2,1,0:T(8,128)} %all-gather.5.cloned.1.call-done) | data formatting | bytes 25165824
  483.9 0.0 copy-done.1
  483.9 0.0 copy-done.2
  (3 shorter events, 0.1 us)
Async XLA Ops:
  7.2 200.0 %copy-start.5 = (bf16[1536,1,1024]{2,0,1:T(8,128)(2,1)S(1)}, bf16[1536,1,1024]{2,0,1:T(8,128)(2,1)}, u32[]{:S(2)}) copy-start(bf16[1536,1,1024]{2,0,1:T(8,128)(2,1)} %param.12) | copy-start | bytes 9437188
  7.2 200.0 %all-gather.3.cloned.1.call-start = ((), (), s32[]{:S(2)}) async-start(), calls=%async_computation.1 | async-start | bytes 10616832 | tf_op jit(solution)/shard_map/all_gather | solution.py:26
  13.3 377.4 %reduce-scatter.2.cloned.1.call-start = ((), (), s32[]{:S(2)}) async-start(), calls=%async_computation.2 | async-start | bytes 12976128 | tf_op jit(solution)/shard_map/reduce_scatter | solution.py:28
  224.6 1.0 copy-start
  224.6 166.0 %copy-start.3 = (f32[1,32,3072]{2,1,0:T(8,128)S(1)}, f32[1,32,3072]{2,1,0:T(8,128)}, u32[]{:S(2)}) copy-start(f32[1,32,3072]{2,1,0:T(8,128)} %param.14) | copy-start | bytes 1179652
  224.6 166.0 %copy-start.4 = (f32[1,32,3072]{2,1,0:T(8,128)S(1)}, f32[1,32,3072]{2,1,0:T(8,128)}, u32[]{:S(2)}) copy-start(f32[1,32,3072]{2,1,0:T(8,128)} %param.15) | copy-start | bytes 1179652
  224.7 248.2 %all-gather.5.cloned.1.call-start = ((), (), s32[]{:S(2)}) async-start(), calls=%async_computation.3 | async-start | bytes 12976128 | tf_op jit(solution)/shard_map/all_gather | solution.py:37
  392.0 91.9 %copy-start.1 = (f32[1,32,3072]{2,1,0:T(8,128)}, f32[1,32,3072]{2,1,0:T(8,128)S(1)}, u32[]{:S(2)}) copy-start(f32[1,32,3072]{2,1,0:T(8,128)S(1)} %get-tuple-element.12) | copy-start | bytes 1179652
  392.1 91.9 %copy-start.2 = (f32[1,32,3072]{2,1,0:T(8,128)}, f32[1,32,3072]{2,1,0:T(8,128)S(1)}, u32[]{:S(2)}) copy-start(f32[1,32,3072]{2,1,0:T(8,128)S(1)} %get-tuple-element.13) | copy-start | bytes 1179652
Sparse Core Ops, SparseCore 0:
  13.4 193.7 all-gather.2
  224.8 165.8 reduce-scatter.1
  393.2 79.6 all-gather.4
where the time goes:
time: 491 us; the launch traced here: 490 us
  waiting for transfers between devices  439 us (89%)
  matrix products  21.3 us (4%)
  between operations  13.8 us (3%)
  local copies, waits for them, and re-layouts  12.1 us (2%)
    all_gather x1, waiting for transfers between devices, local(): everyone = lax.all_gather(dispatched, 'expert', axis=0, tiled=True)  194 us
    reduce_scatter x1, waiting for transfers between devices, local(): grad_slice = lax.psum_scatter(total, 'dp', scatter_dimension=0, tiled=True)  165 us
    all_gather x1, waiting for transfers between devices, local(): gathered = lax.all_gather(new_master, 'dp', axis=1, tiled=True)  79.8 us
    dot_general x1, matrix products, local(): lax.dot_general(hidden, everyone, contract, preferred_element_type=jnp.fl...  17.5 us
    unnamed x13, local copies, waits for them, and re-layouts  11.9 us
  transfers between devices with their start and end apart: 3, of which 3 were waited for; matrix products, arithmetic and copies ran while one was open for 0% of the time, Pallas kernels for 0%

commit v1 on v0

v1 whole, which is shorter than its diff:
```python
import functools

import jax
import jax.numpy as jnp
from jax import lax
from jax.experimental import pallas as pl
from jax.experimental.pallas import tpu as pltpu
from jax.sharding import PartitionSpec as P

MESH = pl.DeviceIdType.MESH
NX, NZ, NC, NY, NH = 4, 4, 2, 4, 2
CHUNKS = 6
AHEAD = 2
LEVELS = 32766.0
LOG2E = 1.4426950408889634
LN2 = 0.6931471805599453


def exponent(top):
    return jnp.floor(jnp.log(jnp.maximum(top, 1e-30)) * LOG2E) + 1.0


def code(x, e):
    return jnp.floor(x * (jnp.exp(e * -LN2) * LEVELS) + 0.5).astype(jnp.int32).astype(jnp.int16)


def scale_of(e16):
    return jnp.exp(e16.astype(jnp.int32).astype(jnp.float32) * LN2) * (1.0 / LEVELS)


def value(q, scale):
    return q.astype(jnp.int32).astype(jnp.float32) * scale


def encode_rows(src, start, rows, dst):
    tile = 32
    width = dst.shape[-1]

    def top(i, m):
        at = pl.multiple_of(start + i * tile, tile)
        return jnp.maximum(m, jnp.abs(src[pl.ds(at, tile), :]))

    m = lax.fori_loop(0, rows // tile, top, jnp.zeros((tile, width), jnp.float32))
    e = exponent(jnp.max(m, axis=0, keepdims=True))

    def put(i, carry):
        at = pl.multiple_of(start + i * tile, tile)
        to = pl.multiple_of(i * tile, tile)
        dst[pl.ds(to, tile), :] = code(src[pl.ds(at, tile), :], e)
        return carry

    lax.fori_loop(0, rows // tile, put, 0)
    dst[pl.ds(rows, 16), :] = jnp.broadcast_to(e, (16, width)).astype(jnp.int32).astype(jnp.int16)


def kernel(ids, probs, gout, gate, up, mas, mo1, mo2, nm_o, m1_o, m2_o, q_o,
           go_v, gate_v, up_v, mas_v, m1_v, m2_v, place, wslot, H, G, acc, pacc, xacc, step_v, ssum,
           csend, crecv, xsend, xrecv, zsend, zrecv, own_q,
           lsem, ssem, rsem, gs, gr):
    dp = lax.axis_index("dp")
    ex = lax.axis_index("expert")
    core, zl, x = dp % NC, (dp // NC) % NZ, dp // (NC * NZ)
    y, zh = ex // NH, ex % NH
    cap = place.shape[0]
    half = cap // 2
    C, _, dc = go_v.shape
    own_rows, D = mas_v.shape

    def at(x_, z_, c_, y_, h_):
        return ((x_ * NZ + z_) * NC + c_, y_ * NH + h_)

    ym, yp = (y + NY - 1) % NY, (y + 1) % NY
    yo = (y + 2) % NY
    dev_z = at(x, zl, core, y, 1 - zh)
    dev_yp, dev_ym = at(x, zl, core, yp, zh), at(x, zl, core, ym, zh)
    dev_c = at(x, zl, 1 - core, y, zh)
    dev_x = [at((x + k) % NX, zl, core, y, zh) for k in range(1, NX)]
    dev_zl = [at(x, (zl + k) % NZ, core, y, zh) for k in range(1, NZ)]
    peers = [dev_z, dev_yp, dev_ym, dev_c] + dev_x + dev_zl

    def local(i):
        if i < C:
            return pltpu.make_async_copy(gout.at[:, pl.ds(i * dc, dc)], go_v.at[i], lsem.at[i])
        src, dst = ((gate, gate_v), (up, up_v), (mas, mas_v), (mo1, m1_v), (mo2, m2_v))[i - C]
        return pltpu.make_async_copy(src, dst, lsem.at[i])

    for i in range(C + 5):
        local(i).start()

    barrier = pltpu.get_barrier_semaphore()
    for dev in peers:
        pl.semaphore_signal(barrier, inc=1, device_id=dev, device_id_type=MESH)

    tokens = ids.shape[1]
    hit0, hit1 = ids[0:1, :] == 0, ids[1:2, :] == 0
    chosen = jnp.where(hit0 | hit1, 1.0, 0.0)
    weight = jnp.where(hit0, probs[0:1, :], 0.0) + jnp.where(hit1, probs[1:2, :], 0.0)
    before = lax.broadcasted_iota(jnp.int32, (tokens, tokens), 0) < lax.broadcasted_iota(jnp.int32, (tokens, tokens), 1)
    count = jnp.dot(
        jnp.broadcast_to(chosen, (16, tokens)).astype(jnp.bfloat16),
        jnp.where(before, 1.0, 0.0).astype(jnp.bfloat16),
        preferred_element_type=jnp.float32,
    )
    slot = jnp.where(chosen > 0.5, count[0:1, :], -1.0)
    mark = lax.broadcasted_iota(jnp.int32, (cap, tokens), 0).astype(jnp.float32) == slot
    place[...] = jnp.where(mark, 1.0, 0.0).astype(jnp.bfloat16)
    wslot[...] = jnp.broadcast_to(jnp.sum(jnp.where(mark, weight, 0.0), axis=1, keepdims=True), wslot.shape)

    def block(c, y_, h_, lo=0, rows=None):
        e = y_ * NH + h_
        return G.at[c, pl.ds(pl.multiple_of(e * cap + lo, 32), cap if rows is None else rows), :]

    def copy(kind, c, src, dst, dev):
        return pltpu.make_async_remote_copy(
            src_ref=src, dst_ref=dst, send_sem=ssem.at[kind, c], recv_sem=rsem.at[kind, c],
            device_id=dev, device_id_type=MESH)

    def gather_copy(kind, c):
        if kind == 0:
            b, dev = block(c, y, zh), dev_z
        elif kind in (1, 2):
            b, dev = block(c, y, zh), (dev_yp if kind == 1 else dev_ym)
        elif kind in (3, 7):
            b, dev = block(c, ym, zh if kind == 3 else 1 - zh, 0, half), dev_yp
        elif kind in (4, 8):
            b, dev = block(c, yp, zh if kind == 4 else 1 - zh, half, half), dev_ym
        else:
            b, dev = block(c, y, 1 - zh), (dev_yp if kind == 5 else dev_ym)
        return copy(kind, c, b, b, dev)

    def gather_arrival(kind, c):
        if kind == 0:
            b = block(c, y, 1 - zh)
        elif kind in (1, 5):
            b = block(c, ym, zh if kind == 1 else 1 - zh)
        elif kind in (2, 6):
            b = block(c, yp, zh if kind == 2 else 1 - zh)
        elif kind in (3, 7):
            b = block(c, yo, zh if kind == 3 else 1 - zh, 0, half)
        else:
            b = block(c, yo, zh if kind == 4 else 1 - zh, half, half)
        return copy(kind, c, b, b, dev_z)

    def core_copy(c):
        return copy(9, c, csend.at[c], crecv.at[c], dev_c)

    def x_copy(c, k):
        return copy(9 + k, c, xsend.at[c, k - 1], xrecv.at[c, k - 1], dev_x[k - 1])

    def z_copy(c, k):
        return copy(12 + k, c, zsend.at[c, k - 1], zrecv.at[c, k - 1], dev_zl[k - 1])

    def fill(c):
        pltpu.make_async_copy(gout.at[:, pl.ds(0, dc)], go_v.at[c], lsem.at[c]).wait()
        rows = jnp.dot(place[...], go_v[c], preferred_element_type=jnp.float32)
        block(c, y, zh)[...] = (rows * wslot[:, 0:1]).astype(jnp.bfloat16)
        for kind in (0, 1, 2):
            gather_copy(kind, c).start()

    fill_first = min(AHEAD, C)
    pl.semaphore_wait(barrier, len(peers))
    for c in range(fill_first):
        fill(c)

    local(C).wait()
    local(C + 1).wait()

    def make_hidden(b, carry):
        cols = pl.ds(pl.multiple_of(b * 128, 128), 128)
        g = gate_v[:, cols].astype(jnp.float32)
        u = up_v[:, cols].astype(jnp.float32)
        h = (g / (1.0 + jnp.exp(-g)) * u).astype(jnp.bfloat16).T
        to = pl.multiple_of(b * 64, 64)
        H[0, pl.ds(to, 32), :] = h[0:32]
        H[1, pl.ds(to, 32), :] = h[32:64]
        H[0, pl.ds(to + 32, 32), :] = h[64:96]
        H[1, pl.ds(to + 32, 32), :] = h[96:128]
        return carry

    lax.fori_loop(0, gate_v.shape[1] // 128, make_hidden, 0)
    for i in range(2, 5):
        local(C + i).wait()
    ssum[...] = jnp.zeros_like(ssum)

    hrows = H.shape[1]
    xrows = hrows // NX
    zrows = xrows // NZ

    def stage_b(c):
        for kind in (1, 2):
            gather_arrival(kind, c).wait_recv()
            gather_copy(kind + 2, c).start()
        gather_arrival(0, c).wait_recv()
        for kind in (5, 6):
            gather_copy(kind, c).start()

    def stage_c(c):
        for kind in (5, 6):
            gather_arrival(kind, c).wait_recv()
            gather_copy(kind + 2, c).start()

    def stage_d(c):
        for kind in (3, 4, 7, 8):
            gather_arrival(kind, c).wait_recv()
        pacc[...] = jnp.dot(H[1 - core], G[c], preferred_element_type=jnp.float32)
        encode_rows(pacc, 0, hrows, csend.at[c])
        core_copy(c).start()
        acc[...] = jnp.dot(H[core], G[c], preferred_element_type=jnp.float32)
        core_copy(c).wait_recv()
        s = scale_of(crecv[c, pl.ds(hrows, 16), :])[0:1]

        def join(i, carry):
            rows = pl.ds(pl.multiple_of(i * 32, 32), 32)
            acc[rows, :] = acc[rows, :] + value(crecv[c, rows, :], s)
            return carry

        lax.fori_loop(0, hrows // 32, join, 0)
        for k in range(1, NX):
            encode_rows(acc, ((x + k) % NX) * xrows, xrows, xsend.at[c, k - 1])
            x_copy(c, k).start()

    def stage_e(c):
        scales = []
        for k in range(1, NX):
            x_copy(c, k).wait_recv()
            scales.append(scale_of(xrecv[c, k - 1, pl.ds(xrows, 16), :])[0:1])

        def join(i, carry):
            rows = pl.ds(pl.multiple_of(i * 32, 32), 32)
            total = acc[pl.ds(pl.multiple_of(x * xrows + i * 32, 32), 32), :]
            for k in range(1, NX):
                total = total + value(xrecv[c, k - 1, rows, :], scales[k - 1])
            xacc[rows, :] = total
            return carry

        lax.fori_loop(0, xrows // 32, join, 0)
        for k in range(1, NZ):
            encode_rows(xacc, ((zl + k) % NZ) * zrows, zrows, zsend.at[c, k - 1])
            z_copy(c, k).start()

    def stage_f(c):
        g = xacc[pl.ds(pl.multiple_of(zl * zrows, zrows), zrows), :]
        for k in range(1, NZ):
            z_copy(c, k).wait_recv()
            s = scale_of(zrecv[c, k - 1, pl.ds(zrows, 16), :])[0:1]
            g = g + value(zrecv[c, k - 1, pl.ds(0, zrows), :], s)
        cols = pl.ds(pl.multiple_of(c * dc, 128), dc)
        one = 0.9 * m1_v[:, cols] + 0.1 * g
        two = 0.95 * m2_v[:, cols] + 0.05 * g * g
        m1_o[:, cols] = one
        m2_o[:, cols] = two
        step = one / (1.0 - 0.9**20) / (jnp.sqrt(two / (1.0 - 0.95**20)) + 1e-08)
        step_v[:, cols] = step
        sq = step * step
        part = sq[:, 0:128]
        for j in range(1, dc // 128):
            part = part + sq[:, j * 128:(j + 1) * 128]
        ssum[...] += part

    def tick(t, carry):
        def guarded(stage, c):
            @pl.when((c >= 0) & (c < C))
            def _():
                stage(c)

        @pl.when(t + AHEAD < C)
        def _():
            fill(t + AHEAD)

        guarded(stage_b, t)
        guarded(stage_c, t - 1)
        guarded(stage_f, t - 4)
        guarded(stage_e, t - 3)
        guarded(stage_d, t - 2)
        return carry

    lax.fori_loop(0, C + 4, tick, 0)

    mas2 = mas_v[...] * mas_v[...]
    wrms = jnp.sqrt(jnp.sum(mas2, axis=1, keepdims=True) / D + 1e-06)
    srms = jnp.sqrt(jnp.sum(ssum[...], axis=1, keepdims=True) / D + 1e-06)
    factor = jnp.minimum(1.0, 0.02 * wrms / (0.01 * srms))
    new = mas_v[...] - 0.01 * factor * step_v[...]
    nm_o[...] = new
    top = jnp.abs(new[:, 0:128])
    for j in range(1, D // 128):
        top = jnp.maximum(top, jnp.abs(new[:, j * 128:(j + 1) * 128]))
    e = exponent(top)
    for j in range(D // 128):
        own_q[:, j * 128:(j + 1) * 128] = code(new[:, j * 128:(j + 1) * 128], e)
    own_q[:, D:D + 128] = e.astype(jnp.int32).astype(jnp.int16)

    def send(i, src, origin, dev):
        return pltpu.make_async_remote_copy(
            src_ref=src, dst_ref=q_o.at[origin], send_sem=gs.at[i], recv_sem=gr.at[i],
            device_id=dev, device_id_type=MESH)

    def home(x_, z_, c_):
        return (x_ * NZ + z_) * NC + c_

    def origin_z(k):
        return home(x, (zl + NZ - k) % NZ, core)

    sent = []

    def go(i, src, origin, dev):
        cp = send(i, src, origin, dev)
        cp.start()
        sent.append(cp)

    keep = pltpu.make_async_copy(own_q, q_o.at[dp], lsem.at[0])
    keep.start()
    for j in range(1, NX):
        go(3 + (j - 1) * 4, own_q, dp, dev_x[j - 1])
    for k in (1, 3, 2):
        go(k - 1, own_q, dp, dev_zl[k - 1])
    go(15, own_q, dp, dev_c)
    for k in (1, 3, 2):
        o = origin_z(k)
        send(k - 1, own_q, o, dev_c).wait_recv()
        for j in range(1, NX):
            go(3 + (j - 1) * 4 + k, q_o.at[o], o, dev_x[j - 1])
        go(15 + k, q_o.at[o], o, dev_c)
    for k in (0, 1, 3, 2):
        for j in (1, 3, 2):
            o = home((x + NX - j) % NX, (zl + NZ - k) % NZ, core)
            send(3 + (j - 1) * 4 + k, own_q, o, dev_c).wait_recv()
            go(15 + j * 4 + k, q_o.at[o], o, dev_c)
    for j in range(NX):
        for k in range(NZ):
            o = home((x + NX - j) % NX, (zl + NZ - k) % NZ, 1 - core)
            send(15 + j * 4 + k, own_q, o, dev_c).wait_recv()
    for cp in sent:
        cp.wait_send()
    keep.wait()

    def drain(c, carry):
        for kind in range(9):
            gather_copy(kind, c).wait_send()
        core_copy(c).wait_send()
        for k in range(1, NX):
            x_copy(c, k).wait_send()
        for k in range(1, NZ):
            z_copy(c, k).wait_send()
        return carry

    lax.fori_loop(0, C, drain, 0)


def decode(q_ref, a_ref, b_ref, c_ref, o_ref, a_o, b_o, c_o):
    blocks, rows, width = q_ref.shape

    @pl.when(pl.program_id(0) == 0)
    def _():
        a_o[...] = a_ref[...]
        b_o[...] = b_ref[...]
        c_o[...] = c_ref[...]

    for b in range(blocks):
        s = scale_of(q_ref[b, :, width - 128:])
        for j in range((width - 128) // 128):
            cols = slice(j * 128, (j + 1) * 128)
            o_ref[pl.ds(b * rows, rows), cols] = value(q_ref[b, :, cols], s)


def local(grad_out, expert_ids, gate_probs, saved_gate, saved_up, master, moment_one, moment_two):
    tokens, D = grad_out.shape
    cap = tokens * 3 // 8
    slots, _, width = saved_gate.shape
    rows = master.shape[1]
    devices = NX * NZ * NC
    C, dc = CHUNKS, D // CHUNKS
    f32, bf16, i16 = jnp.float32, jnp.bfloat16, jnp.int16
    vm = pl.BlockSpec(memory_space=pltpu.VMEM)
    hbm = pl.BlockSpec(memory_space=pl.ANY)
    hrows = width // NC
    xrows = hrows // NX
    outs = pl.pallas_call(
        kernel,
        name="step",
        out_shape=(
            jax.ShapeDtypeStruct((rows, D), f32),
            jax.ShapeDtypeStruct((rows, D), f32),
            jax.ShapeDtypeStruct((rows, D), f32),
            jax.ShapeDtypeStruct((devices, rows, D + 128), i16),
        ),
        in_specs=[vm, vm] + [hbm] * 6,
        out_specs=(vm, vm, vm, hbm),
        scratch_shapes=[
            pltpu.VMEM((C, tokens, dc), bf16),
            pltpu.VMEM((slots, width), bf16),
            pltpu.VMEM((slots, width), bf16),
            pltpu.VMEM((rows, D), f32),
            pltpu.VMEM((rows, D), f32),
            pltpu.VMEM((rows, D), f32),
            pltpu.VMEM((cap, tokens), bf16),
            pltpu.VMEM((cap, 128), f32),
            pltpu.VMEM((NC, hrows, slots), bf16),
            pltpu.VMEM((C, slots, dc), bf16),
            pltpu.VMEM((hrows, dc), f32),
            pltpu.VMEM((hrows, dc), f32),
            pltpu.VMEM((xrows, dc), f32),
            pltpu.VMEM((rows, D), f32),
            pltpu.VMEM((rows, 128), f32),
            pltpu.VMEM((C, hrows + 16, dc), i16),
            pltpu.VMEM((C, hrows + 16, dc), i16),
            pltpu.VMEM((C, NX - 1, xrows + 16, dc), i16),
            pltpu.VMEM((C, NX - 1, xrows + 16, dc), i16),
            pltpu.VMEM((C, NZ - 1, rows + 16, dc), i16),
            pltpu.VMEM((C, NZ - 1, rows + 16, dc), i16),
            pltpu.VMEM((rows, D + 128), i16),
            pltpu.SemaphoreType.DMA((C + 5,)),
            pltpu.SemaphoreType.DMA((16, C)),
            pltpu.SemaphoreType.DMA((16, C)),
            pltpu.SemaphoreType.DMA((31,)),
            pltpu.SemaphoreType.DMA((31,)),
        ],
        compiler_params=pltpu.CompilerParams(
            collective_id=0, has_side_effects=True, vmem_limit_bytes=60 << 20),
    )(
        expert_ids.T, gate_probs.T, grad_out,
        saved_gate.reshape(slots, width), saved_up.reshape(slots, width),
        master.reshape(rows, D), moment_one.reshape(rows, D), moment_two.reshape(rows, D),
    )
    new, one, two, q = outs
    per = 2
    whole = pl.BlockSpec((rows, D), lambda i: (0, 0))
    full, new, one, two = pl.pallas_call(
        decode,
        name="decode",
        grid=(devices // per,),
        out_shape=(jax.ShapeDtypeStruct((devices * rows, D), f32),) + (jax.ShapeDtypeStruct((rows, D), f32),) * 3,
        in_specs=[pl.BlockSpec((per, rows, D + 128), lambda i: (i, 0, 0)), whole, whole, whole],
        out_specs=(pl.BlockSpec((per * rows, D), lambda i: (i, 0)), whole, whole, whole),
    )(q, new, one, two)
    shape = master.shape
    return (new.reshape(shape), one.reshape(shape), two.reshape(shape), full.reshape(1, devices * rows, D))


def solution(mesh):
    return jax.shard_map(
        local,
        mesh=mesh,
        in_specs=(
            P(("dp", "expert"), None),
            P(("dp", "expert"), None),
            P(("dp", "expert"), None),
            P("dp", "expert", None),
            P("dp", "expert", None),
            P("expert", "dp", None),
            P("expert", "dp", None),
            P("expert", "dp", None),
        ),
        out_specs=(
            P("expert", "dp", None),
            P("expert", "dp", None),
            P("expert", "dp", None),
            P("expert", None, None),
        ),
        check_vma=False,
    )
```

time: 491 us -> 188 us (0.38)
  waiting for transfers between devices: 439 us -> 0 us
  Pallas kernels: 0 us -> 187 us
  matrix products: 21.3 us -> 0 us
  between operations: 13.8 us -> 0.64 us
  local copies, waits for them, and re-layouts: 12.1 us -> 0 us
    all_gather x2 -> x0, waiting for transfers between devices: 274 us -> none  [the longest x1 194 us: local(): everyone = lax.all_gather(dispatched, 'expert', axis=0, tiled=True)]
    pallas_call x0 -> x2, Pallas kernels: none -> 187 us  [the longest x1 174 us: local(): pl.pallas_call(kernel, name='step', out_shape=(jax.ShapeDtypeStruct((rows...]
    reduce_scatter x1 -> x0, waiting for transfers between devices: 165 us -> none  [local(): grad_slice = lax.psum_scatter(total, 'dp', scatter_dimension=0, tiled=True)]
    dot_general x2 -> x0, matrix products: 21.3 us -> none  [the longest x1 17.5 us: local(): lax.dot_general(hidden, everyone, contract, preferred_element_type=jnp.fl...]
    unnamed x13 -> x0, local copies, waits for them, and re-layouts: 11.9 us -> none
  transfers between devices with their start and end apart: 3 -> 0, of which waited for: 3 -> 0; matrix products, arithmetic and copies ran while one was open for 0% -> 0% of each run, Pallas kernels for 0% -> 0%
where the time goes in v1:
time: 188 us
  Pallas kernels  187 us (99%)
    pallas_call x1, Pallas kernels, local(): pl.pallas_call(kernel, name='step', out_shape=(jax.ShapeDtypeStruct((rows...  174 us
    pallas_call x1, Pallas kernels, local(): pl.pallas_call(decode, name='decode', grid=(devices // per,), out_shape=(...  13.2 us

profile of v1, /device:TPU:1, one launch (start us, length us, event | category | flops | bytes accessed | tf_op | source)
XLA Modules:
  0.0 187.6 jit_solution(15295729801184159358)
XLA Ops:
  0.6 173.8 %step.1 = (f32[32,3072]{1,0:T(8,128)}, f32[32,3072]{1,0:T(8,128)}, f32[32,3072]{1,0:T(8,128)}, s16[32,32,3200]{2,1,0:T(8,128)(2,1)}) custom-call(s32[2,512]{1,0:T(2,128)} %bitcast.16, f32[2,512]{1,0:T(2,128)} %bitcast.17, bf16[512,3072]{1,0:T(8,128)(2,1)} %gout.1, bf16[1536,1024]{1,0:T(8,128)(2,1)} %bitcast.11, bf16[1536,1024]{1,0:T(8,128)(2,1)} %bitcast.12, ...), custom_call_target="tpu_custom_call" | custom-call | tf_op jit(solution)/shard_map/step/pallas_call | solution.py:378
  174.5 13.2 %decode.1 = (f32[1024,3072]{1,0:T(8,128)}, f32[32,3072]{1,0:T(8,128)}, f32[32,3072]{1,0:T(8,128)}, f32[32,3072]{1,0:T(8,128)}) custom-call(s16[32,32,3200]{2,1,0:T(8,128)(2,1)} %get-tuple-element.12.q_ref, f32[32,3072]{1,0:T(8,128)} %get-tuple-element.13.a_ref, f32[32,3072]{1,0:T(8,128)} %get-tuple-element.14.b_ref, f32[32,3072]{1,0:T(8,128)} %get-tuple-element.15.c_ref), custom_call_target="tpu_custom_call" | custom-call | tf_op jit(solution)/shard_map/decode/pallas_call | solution.py:428

commit v2 on v1

--- a/solution.py
+++ b/solution.py
@@ -9,8 +9,10 @@
 
 MESH = pl.DeviceIdType.MESH
 NX, NZ, NC, NY, NH = 4, 4, 2, 4, 2
-CHUNKS = 6
-AHEAD = 2
+CHUNKS = 8
+AHEAD = 3
+TILE = 32
+LAG_E, LAG_F = 4, 6
 LEVELS = 32766.0
 LOG2E = 1.4426950408889634
 LN2 = 0.6931471805599453
@@ -20,41 +22,27 @@
     return jnp.floor(jnp.log(jnp.maximum(top, 1e-30)) * LOG2E) + 1.0
 
 
-def code(x, e):
-    return jnp.floor(x * (jnp.exp(e * -LN2) * LEVELS) + 0.5).astype(jnp.int32).astype(jnp.int16)
-
-
-def scale_of(e16):
-    return jnp.exp(e16.astype(jnp.int32).astype(jnp.float32) * LN2) * (1.0 / LEVELS)
-
-
-def value(q, scale):
-    return q.astype(jnp.int32).astype(jnp.float32) * scale
-
-
-def encode_rows(src, start, rows, dst):
-    tile = 32
-    width = dst.shape[-1]
-
-    def top(i, m):
-        at = pl.multiple_of(start + i * tile, tile)
-        return jnp.maximum(m, jnp.abs(src[pl.ds(at, tile), :]))
-
-    m = lax.fori_loop(0, rows // tile, top, jnp.zeros((tile, width), jnp.float32))
-    e = exponent(jnp.max(m, axis=0, keepdims=True))
-
-    def put(i, carry):
-        at = pl.multiple_of(start + i * tile, tile)
-        to = pl.multiple_of(i * tile, tile)
-        dst[pl.ds(to, tile), :] = code(src[pl.ds(at, tile), :], e)
-        return carry
-
-    lax.fori_loop(0, rows // tile, put, 0)
-    dst[pl.ds(rows, 16), :] = jnp.broadcast_to(e, (16, width)).astype(jnp.int32).astype(jnp.int16)
+def encode(x, dst, rows):
+    n = x.shape[-1] // 128
+    parts = [x[:, j * 128:(j + 1) * 128] for j in range(n)]
+    top = jnp.abs(parts[0])
+    for p in parts[1:]:
+        top = jnp.maximum(top, jnp.abs(p))
+    e = exponent(top)
+    s = jnp.exp(e * -LN2) * LEVELS
+    for j, p in enumerate(parts):
+        dst[rows, j * 128:(j + 1) * 128] = jnp.floor(p * s + 0.5).astype(jnp.int32).astype(jnp.int16)
+    dst[rows, n * 128:] = e.astype(jnp.int32).astype(jnp.int16)
+
+
+def decoded(src, rows):
+    n = src.shape[-1] // 128 - 1
+    s = jnp.exp(src[rows, n * 128:].astype(jnp.int32).astype(jnp.float32) * LN2) * (1.0 / LEVELS)
+    return [src[rows, j * 128:(j + 1) * 128].astype(jnp.int32).astype(jnp.float32) * s for j in range(n)]
 
 
 def kernel(ids, probs, gout, gate, up, mas, mo1, mo2, nm_o, m1_o, m2_o, q_o,
-           go_v, gate_v, up_v, mas_v, m1_v, m2_v, place, wslot, H, G, acc, pacc, xacc, step_v, ssum,
+           go_v, gate_v, up_v, mas_v, m1_v, m2_v, place, wslot, H, G, acc, xacc, step_v, ssum,
            csend, crecv, xsend, xrecv, zsend, zrecv, own_q,
            lsem, ssem, rsem, gs, gr):
     dp = lax.axis_index("dp")
@@ -202,48 +190,53 @@
     def stage_d(c):
         for kind in (3, 4, 7, 8):
             gather_arrival(kind, c).wait_recv()
-        pacc[...] = jnp.dot(H[1 - core], G[c], preferred_element_type=jnp.float32)
-        encode_rows(pacc, 0, hrows, csend.at[c])
+        csend[c] = jnp.dot(H[1 - core], G[c], preferred_element_type=jnp.float32)
         core_copy(c).start()
         acc[...] = jnp.dot(H[core], G[c], preferred_element_type=jnp.float32)
         core_copy(c).wait_recv()
-        s = scale_of(crecv[c, pl.ds(hrows, 16), :])[0:1]
+        for k in (2, 1, 3):
+            base = ((x + k) % NX) * xrows
+
+            def put(i, carry):
+                rows = pl.ds(pl.multiple_of(base + i * TILE, TILE), TILE)
+                encode(acc[rows, :] + crecv[c, rows, :], xsend.at[c, k - 1],
+                       pl.ds(pl.multiple_of(i * TILE, TILE), TILE))
+                return carry
+
+            lax.fori_loop(0, xrows // TILE, put, 0)
+            x_copy(c, k).start()
+
+        own = pl.ds(pl.multiple_of(x * xrows, xrows), xrows)
+        xacc[c] = acc[own, :] + crecv[c, own, :]
+
+    def stage_e(c):
+        for k in (1, 3, 2):
+            x_copy(c, k).wait_recv()
 
         def join(i, carry):
-            rows = pl.ds(pl.multiple_of(i * 32, 32), 32)
-            acc[rows, :] = acc[rows, :] + value(crecv[c, rows, :], s)
+            rows = pl.ds(pl.multiple_of(i * TILE, TILE), TILE)
+            got = [decoded(xrecv.at[c, k - 1], rows) for k in range(1, NX)]
+            for j in range(dc // 128):
+                cols = slice(j * 128, (j + 1) * 128)
+                total = xacc[c, rows, cols]
+                for g in got:
+                    total = total + g[j]
+                xacc[c, rows, cols] = total
             return carry
 
-        lax.fori_loop(0, hrows // 32, join, 0)
-        for k in range(1, NX):
-            encode_rows(acc, ((x + k) % NX) * xrows, xrows, xsend.at[c, k - 1])
-            x_copy(c, k).start()
-
-    def stage_e(c):
-        scales = []
-        for k in range(1, NX):
-            x_copy(c, k).wait_recv()
-            scales.append(scale_of(xrecv[c, k - 1, pl.ds(xrows, 16), :])[0:1])
-
-        def join(i, carry):
-            rows = pl.ds(pl.multiple_of(i * 32, 32), 32)
-            total = acc[pl.ds(pl.multiple_of(x * xrows + i * 32, 32), 32), :]
-            for k in range(1, NX):
-                total = total + value(xrecv[c, k - 1, rows, :], scales[k - 1])
-            xacc[rows, :] = total
-            return carry
-
-        lax.fori_loop(0, xrows // 32, join, 0)
-        for k in range(1, NZ):
-            encode_rows(xacc, ((zl + k) % NZ) * zrows, zrows, zsend.at[c, k - 1])
+        lax.fori_loop(0, xrows // TILE, join, 0)
+        every = pl.ds(0, zrows)
+        for k in (2, 1, 3):
+            encode(xacc[c, pl.ds(pl.multiple_of(((zl + k) % NZ) * zrows, zrows), zrows), :], zsend.at[c, k - 1], every)
             z_copy(c, k).start()
 
     def stage_f(c):
-        g = xacc[pl.ds(pl.multiple_of(zl * zrows, zrows), zrows), :]
-        for k in range(1, NZ):
+        for k in (1, 3, 2):
             z_copy(c, k).wait_recv()
-            s = scale_of(zrecv[c, k - 1, pl.ds(zrows, 16), :])[0:1]
-            g = g + value(zrecv[c, k - 1, pl.ds(0, zrows), :], s)
+        g = xacc[c, pl.ds(pl.multiple_of(zl * zrows, zrows), zrows), :]
+        got = [jnp.concatenate(decoded(zrecv.at[c, k - 1], pl.ds(0, zrows)), axis=1) for k in range(1, NZ)]
+        for part in got:
+            g = g + part
         cols = pl.ds(pl.multiple_of(c * dc, 128), dc)
         one = 0.9 * m1_v[:, cols] + 0.1 * g
         two = 0.95 * m2_v[:, cols] + 0.05 * g * g
@@ -269,12 +262,12 @@
 
         guarded(stage_b, t)
         guarded(stage_c, t - 1)
-        guarded(stage_f, t - 4)
-        guarded(stage_e, t - 3)
+        guarded(stage_f, t - LAG_F)
+        guarded(stage_e, t - LAG_E)
         guarded(stage_d, t - 2)
         return carry
 
-    lax.fori_loop(0, C + 4, tick, 0)
+    lax.fori_loop(0, C + LAG_F, tick, 0)
 
     mas2 = mas_v[...] * mas_v[...]
     wrms = jnp.sqrt(jnp.sum(mas2, axis=1, keepdims=True) / D + 1e-06)
@@ -282,54 +275,73 @@
     factor = jnp.minimum(1.0, 0.02 * wrms / (0.01 * srms))
     new = mas_v[...] - 0.01 * factor * step_v[...]
     nm_o[...] = new
-    top = jnp.abs(new[:, 0:128])
-    for j in range(1, D // 128):
-        top = jnp.maximum(top, jnp.abs(new[:, j * 128:(j + 1) * 128]))
-    e = exponent(top)
-    for j in range(D // 128):
-        own_q[:, j * 128:(j + 1) * 128] = code(new[:, j * 128:(j + 1) * 128], e)
-    own_q[:, D:D + 128] = e.astype(jnp.int32).astype(jnp.int16)
-
-    def send(i, src, origin, dev):
+    encode(new, own_q, pl.ds(0, own_rows))
+
+    low = own_rows // 2
+    dev_xp, dev_xm = dev_x[0], dev_x[NX - 2]
+
+    def home(x_, z_, c_):
+        return ((x_ % NX) * NZ + z_ % NZ) * NC + c_
+
+    def piece(origin, part):
+        if part is None:
+            return q_o.at[origin]
+        return q_o.at[origin, pl.ds(part * low, low), :]
+
+    def send(i, src, dst, dev):
         return pltpu.make_async_remote_copy(
-            src_ref=src, dst_ref=q_o.at[origin], send_sem=gs.at[i], recv_sem=gr.at[i],
-            device_id=dev, device_id_type=MESH)
-
-    def home(x_, z_, c_):
-        return (x_ * NZ + z_) * NC + c_
-
-    def origin_z(k):
-        return home(x, (zl + NZ - k) % NZ, core)
+            src_ref=src, dst_ref=dst, send_sem=gs.at[i], recv_sem=gr.at[i], device_id=dev, device_id_type=MESH)
 
     sent = []
 
-    def go(i, src, origin, dev):
-        cp = send(i, src, origin, dev)
+    def go(i, src, dst, dev):
+        cp = send(i, src, dst, dev)
         cp.start()
         sent.append(cp)
 
+    def arrived(i, dst):
+        send(i, dst, dst, dev_c).wait_recv()
+
+    Z0, XR, XF, CR = 0, 3, 11, 19
+
+    def from_z(k):
+        o = home(x, zl + NZ - k, core)
+        arrived(Z0 + k - 1, piece(o, None))
+        for d, dev in ((0, dev_xp), (1, dev_xm)):
+            go(XR + d * 4 + k, piece(o, None), piece(o, None), dev)
+        go(CR + k, piece(o, None), piece(o, None), dev_c)
+
+    def from_x(k):
+        for d, (off, dev) in enumerate(((NX - 1, dev_xp), (1, dev_xm))):
+            o = home(x + off, zl + NZ - k, core)
+            arrived(XR + d * 4 + k, piece(o, None))
+            go(XF + d * 4 + k, piece(o, d), piece(o, d), dev)
+            go(CR + off * 4 + k, piece(o, None), piece(o, None), dev_c)
+
+    def from_far(k):
+        o = home(x + 2, zl + NZ - k, core)
+        for d in (0, 1):
+            arrived(XF + d * 4 + k, piece(o, d))
+        go(CR + 2 * 4 + k, piece(o, None), piece(o, None), dev_c)
+
     keep = pltpu.make_async_copy(own_q, q_o.at[dp], lsem.at[0])
     keep.start()
-    for j in range(1, NX):
-        go(3 + (j - 1) * 4, own_q, dp, dev_x[j - 1])
+    go(XR, own_q, q_o.at[dp], dev_xp)
+    go(XR + 4, own_q, q_o.at[dp], dev_xm)
     for k in (1, 3, 2):
-        go(k - 1, own_q, dp, dev_zl[k - 1])
-    go(15, own_q, dp, dev_c)
+        go(Z0 + k - 1, own_q, q_o.at[dp], dev_zl[k - 1])
+    go(CR, own_q, q_o.at[dp], dev_c)
+    from_z(1)
+    from_z(3)
+    from_x(0)
+    from_z(2)
     for k in (1, 3, 2):
-        o = origin_z(k)
-        send(k - 1, own_q, o, dev_c).wait_recv()
-        for j in range(1, NX):
-            go(3 + (j - 1) * 4 + k, q_o.at[o], o, dev_x[j - 1])
-        go(15 + k, q_o.at[o], o, dev_c)
+        from_x(k)
     for k in (0, 1, 3, 2):
-        for j in (1, 3, 2):
-            o = home((x + NX - j) % NX, (zl + NZ - k) % NZ, core)
-            send(3 + (j - 1) * 4 + k, own_q, o, dev_c).wait_recv()
-            go(15 + j * 4 + k, q_o.at[o], o, dev_c)
-    for j in range(NX):
+        from_far(k)
+    for off in (0, 1, 3, 2):
         for k in range(NZ):
-            o = home((x + NX - j) % NX, (zl + NZ - k) % NZ, 1 - core)
-            send(15 + j * 4 + k, own_q, o, dev_c).wait_recv()
+            arrived(CR + off * 4 + k, piece(home(x + off, zl + NZ - k, 1 - core), None))
     for cp in sent:
         cp.wait_send()
     keep.wait()
@@ -357,10 +369,8 @@
         c_o[...] = c_ref[...]
 
     for b in range(blocks):
-        s = scale_of(q_ref[b, :, width - 128:])
-        for j in range((width - 128) // 128):
-            cols = slice(j * 128, (j + 1) * 128)
-            o_ref[pl.ds(b * rows, rows), cols] = value(q_ref[b, :, cols], s)
+        for j, part in enumerate(decoded(q_ref.at[b], pl.ds(0, rows))):
+            o_ref[pl.ds(b * rows, rows), j * 128:(j + 1) * 128] = part
 
 
 def local(grad_out, expert_ids, gate_probs, saved_gate, saved_up, master, moment_one, moment_two):
@@ -398,22 +408,21 @@
             pltpu.VMEM((NC, hrows, slots), bf16),
             pltpu.VMEM((C, slots, dc), bf16),
             pltpu.VMEM((hrows, dc), f32),
-            pltpu.VMEM((hrows, dc), f32),
-            pltpu.VMEM((xrows, dc), f32),
+            pltpu.VMEM((C, xrows, dc), f32),
             pltpu.VMEM((rows, D), f32),
             pltpu.VMEM((rows, 128), f32),
-            pltpu.VMEM((C, hrows + 16, dc), i16),
-            pltpu.VMEM((C, hrows + 16, dc), i16),
-            pltpu.VMEM((C, NX - 1, xrows + 16, dc), i16),
-            pltpu.VMEM((C, NX - 1, xrows + 16, dc), i16),
-            pltpu.VMEM((C, NZ - 1, rows + 16, dc), i16),
-            pltpu.VMEM((C, NZ - 1, rows + 16, dc), i16),
+            pltpu.VMEM((C, hrows, dc), f32),
+            pltpu.VMEM((C, hrows, dc), f32),
+            pltpu.VMEM((C, NX - 1, xrows, dc + 128), i16),
+            pltpu.VMEM((C, NX - 1, xrows, dc + 128), i16),
+            pltpu.VMEM((C, NZ - 1, rows, dc + 128), i16),
+            pltpu.VMEM((C, NZ - 1, rows, dc + 128), i16),
             pltpu.VMEM((rows, D + 128), i16),
             pltpu.SemaphoreType.DMA((C + 5,)),
             pltpu.SemaphoreType.DMA((16, C)),
             pltpu.SemaphoreType.DMA((16, C)),
-            pltpu.SemaphoreType.DMA((31,)),
-            pltpu.SemaphoreType.DMA((31,)),
+            pltpu.SemaphoreType.DMA((35,)),
+            pltpu.SemaphoreType.DMA((35,)),
         ],
         compiler_params=pltpu.CompilerParams(
             collective_id=0, has_side_effects=True, vmem_limit_bytes=60 << 20),
@@ -423,7 +432,7 @@
         master.reshape(rows, D), moment_one.reshape(rows, D), moment_two.reshape(rows, D),
     )
     new, one, two, q = outs
-    per = 2
+    per = 8
     whole = pl.BlockSpec((rows, D), lambda i: (0, 0))
     full, new, one, two = pl.pallas_call(
         decode,

time: 188 us -> 158 us (0.84)
  Pallas kernels: 187 us -> 157 us
    pallas_call x1, Pallas kernels: 174 us -> 148 us  [local(): pl.pallas_call(kernel, name='step', out_shape=(jax.ShapeDtypeStruct((rows...]
    pallas_call x1, Pallas kernels: 13.2 us -> 8.71 us  [local(): pl.pallas_call(decode, name='decode', grid=(devices // per,), out_shape=(...]
where the time goes in v2:
time: 158 us
  Pallas kernels  157 us (99%)
    pallas_call x1, Pallas kernels, local(): pl.pallas_call(kernel, name='step', out_shape=(jax.ShapeDtypeStruct((rows...  148 us
    pallas_call x1, Pallas kernels, local(): pl.pallas_call(decode, name='decode', grid=(devices // per,), out_shape=(...  8.71 us

profile of v2, /device:TPU:1, one launch (start us, length us, event | category | flops | bytes accessed | tf_op | source)
XLA Modules:
  0.0 157.8 jit_solution(5526266640357949551)
XLA Ops:
  0.6 148.4 %step.1 = (f32[32,3072]{1,0:T(8,128)}, f32[32,3072]{1,0:T(8,128)}, f32[32,3072]{1,0:T(8,128)}, s16[32,32,3200]{2,1,0:T(8,128)(2,1)}) custom-call(s32[2,512]{1,0:T(2,128)} %bitcast.16, f32[2,512]{1,0:T(2,128)} %bitcast.17, bf16[512,3072]{1,0:T(8,128)(2,1)} %gout.1, bf16[1536,1024]{1,0:T(8,128)(2,1)} %bitcast.11, bf16[1536,1024]{1,0:T(8,128)(2,1)} %bitcast.12, ...), custom_call_target="tpu_custom_call" | custom-call | tf_op jit(solution)/shard_map/step/pallas_call | solution.py:388
  149.1 8.7 %decode.1 = (f32[1024,3072]{1,0:T(8,128)}, f32[32,3072]{1,0:T(8,128)}, f32[32,3072]{1,0:T(8,128)}, f32[32,3072]{1,0:T(8,128)}) custom-call(s16[32,32,3200]{2,1,0:T(8,128)(2,1)} %get-tuple-element.12.q_ref, f32[32,3072]{1,0:T(8,128)} %get-tuple-element.13.a_ref, f32[32,3072]{1,0:T(8,128)} %get-tuple-element.14.b_ref, f32[32,3072]{1,0:T(8,128)} %get-tuple-element.15.c_ref), custom_call_target="tpu_custom_call" | custom-call | tf_op jit(solution)/shard_map/decode/pallas_call | solution.py:437

commit v3 on v2

--- a/solution.py
+++ b/solution.py
@@ -9,10 +9,10 @@
 
 MESH = pl.DeviceIdType.MESH
 NX, NZ, NC, NY, NH = 4, 4, 2, 4, 2
-CHUNKS = 8
-AHEAD = 3
+CHUNKS = 12
+AHEAD = 4
 TILE = 32
-LAG_E, LAG_F = 4, 6
+LAG_R, LAG_E, LAG_F = 3, 5, 7
 LEVELS = 32766.0
 LOG2E = 1.4426950408889634
 LN2 = 0.6931471805599453
@@ -72,7 +72,8 @@
         src, dst = ((gate, gate_v), (up, up_v), (mas, mas_v), (mo1, m1_v), (mo2, m2_v))[i - C]
         return pltpu.make_async_copy(src, dst, lsem.at[i])
 
-    for i in range(C + 5):
+    fill_first = min(AHEAD, C)
+    for i in range(fill_first):
         local(i).start()
 
     barrier = pltpu.get_barrier_semaphore()
@@ -145,10 +146,12 @@
         for kind in (0, 1, 2):
             gather_copy(kind, c).start()
 
-    fill_first = min(AHEAD, C)
     pl.semaphore_wait(barrier, len(peers))
     for c in range(fill_first):
         fill(c)
+        if c == 0:
+            for i in [C, C + 1] + list(range(fill_first, C)) + [C + 2, C + 3, C + 4]:
+                local(i).start()
 
     local(C).wait()
     local(C + 1).wait()
@@ -192,14 +195,16 @@
             gather_arrival(kind, c).wait_recv()
         csend[c] = jnp.dot(H[1 - core], G[c], preferred_element_type=jnp.float32)
         core_copy(c).start()
-        acc[...] = jnp.dot(H[core], G[c], preferred_element_type=jnp.float32)
+        acc[c % 2] = jnp.dot(H[core], G[c], preferred_element_type=jnp.float32)
+
+    def stage_r(c):
         core_copy(c).wait_recv()
         for k in (2, 1, 3):
             base = ((x + k) % NX) * xrows
 
             def put(i, carry):
                 rows = pl.ds(pl.multiple_of(base + i * TILE, TILE), TILE)
-                encode(acc[rows, :] + crecv[c, rows, :], xsend.at[c, k - 1],
+                encode(acc[c % 2, rows, :] + crecv[c, rows, :], xsend.at[c, k - 1],
                        pl.ds(pl.multiple_of(i * TILE, TILE), TILE))
                 return carry
 
@@ -207,7 +212,7 @@
             x_copy(c, k).start()
 
         own = pl.ds(pl.multiple_of(x * xrows, xrows), xrows)
-        xacc[c] = acc[own, :] + crecv[c, own, :]
+        xacc[c] = acc[c % 2, own, :] + crecv[c, own, :]
 
     def stage_e(c):
         for k in (1, 3, 2):
@@ -264,6 +269,7 @@
         guarded(stage_c, t - 1)
         guarded(stage_f, t - LAG_F)
         guarded(stage_e, t - LAG_E)
+        guarded(stage_r, t - LAG_R)
         guarded(stage_d, t - 2)
         return carry
 
@@ -324,13 +330,14 @@
             arrived(XF + d * 4 + k, piece(o, d))
         go(CR + 2 * 4 + k, piece(o, None), piece(o, None), dev_c)
 
-    keep = pltpu.make_async_copy(own_q, q_o.at[dp], lsem.at[0])
-    keep.start()
     go(XR, own_q, q_o.at[dp], dev_xp)
     go(XR + 4, own_q, q_o.at[dp], dev_xm)
     for k in (1, 3, 2):
         go(Z0 + k - 1, own_q, q_o.at[dp], dev_zl[k - 1])
     go(CR, own_q, q_o.at[dp], dev_c)
+    kept = [pltpu.make_async_copy(own_q, q_o.at[dp], lsem.at[0])]
+    for cp in kept:
+        cp.start()
     from_z(1)
     from_z(3)
     from_x(0)
@@ -344,7 +351,8 @@
             arrived(CR + off * 4 + k, piece(home(x + off, zl + NZ - k, 1 - core), None))
     for cp in sent:
         cp.wait_send()
-    keep.wait()
+    for cp in kept:
+        cp.wait()
 
     def drain(c, carry):
         for kind in range(9):
@@ -368,8 +376,9 @@
         b_o[...] = b_ref[...]
         c_o[...] = c_ref[...]
 
+    blocks = o_ref.shape[0] // rows
     for b in range(blocks):
-        for j, part in enumerate(decoded(q_ref.at[b], pl.ds(0, rows))):
+        for j, part in enumerate(decoded(q_ref.at[pl.program_id(0) * blocks + b], pl.ds(0, rows))):
             o_ref[pl.ds(b * rows, rows), j * 128:(j + 1) * 128] = part
 
 
@@ -389,13 +398,13 @@
         kernel,
         name="step",
         out_shape=(
-            jax.ShapeDtypeStruct((rows, D), f32),
-            jax.ShapeDtypeStruct((rows, D), f32),
-            jax.ShapeDtypeStruct((rows, D), f32),
-            jax.ShapeDtypeStruct((devices, rows, D + 128), i16),
+            pltpu.VMEM((rows, D), f32),
+            pltpu.VMEM((rows, D), f32),
+            pltpu.VMEM((rows, D), f32),
+            pltpu.VMEM((devices, rows, D + 128), i16),
         ),
         in_specs=[vm, vm] + [hbm] * 6,
-        out_specs=(vm, vm, vm, hbm),
+        out_specs=(vm, vm, vm, vm),
         scratch_shapes=[
             pltpu.VMEM((C, tokens, dc), bf16),
             pltpu.VMEM((slots, width), bf16),
@@ -407,7 +416,7 @@
             pltpu.VMEM((cap, 128), f32),
             pltpu.VMEM((NC, hrows, slots), bf16),
             pltpu.VMEM((C, slots, dc), bf16),
-            pltpu.VMEM((hrows, dc), f32),
+            pltpu.VMEM((2, hrows, dc), f32),
             pltpu.VMEM((C, xrows, dc), f32),
             pltpu.VMEM((rows, D), f32),
             pltpu.VMEM((rows, 128), f32),
@@ -425,22 +434,23 @@
             pltpu.SemaphoreType.DMA((35,)),
         ],
         compiler_params=pltpu.CompilerParams(
-            collective_id=0, has_side_effects=True, vmem_limit_bytes=60 << 20),
+            collective_id=0, has_side_effects=True, vmem_limit_bytes=54 << 20),
     )(
         expert_ids.T, gate_probs.T, grad_out,
         saved_gate.reshape(slots, width), saved_up.reshape(slots, width),
         master.reshape(rows, D), moment_one.reshape(rows, D), moment_two.reshape(rows, D),
     )
     new, one, two, q = outs
-    per = 8
+    per = 4
     whole = pl.BlockSpec((rows, D), lambda i: (0, 0))
     full, new, one, two = pl.pallas_call(
         decode,
         name="decode",
         grid=(devices // per,),
         out_shape=(jax.ShapeDtypeStruct((devices * rows, D), f32),) + (jax.ShapeDtypeStruct((rows, D), f32),) * 3,
-        in_specs=[pl.BlockSpec((per, rows, D + 128), lambda i: (i, 0, 0)), whole, whole, whole],
+        in_specs=[vm, vm, vm, vm],
         out_specs=(pl.BlockSpec((per * rows, D), lambda i: (i, 0)), whole, whole, whole),
+        compiler_params=pltpu.CompilerParams(vmem_limit_bytes=24 << 20),
     )(q, new, one, two)
     shape = master.shape
     return (new.reshape(shape), one.reshape(shape), two.reshape(shape), full.reshape(1, devices * rows, D))

time: 158 us -> 151 us (0.956)
  Pallas kernels: 157 us -> 149 us
    pallas_call x1, Pallas kernels: 148 us -> 143 us  [local(): pl.pallas_call(kernel, name='step', out_shape=(pltpu.VMEM((rows, D), f32)...]
    pallas_call x1, Pallas kernels: 8.71 us -> 6.17 us  [local(): pl.pallas_call(decode, name='decode', grid=(devices // per,), out_shape=(...]
where the time goes in v3:
time: 151 us; the launch traced here: 150 us
  Pallas kernels  149 us (99%)
    pallas_call x1, Pallas kernels, local(): pl.pallas_call(kernel, name='step', out_shape=(pltpu.VMEM((rows, D), f32)...  143 us
    pallas_call x1, Pallas kernels, local(): pl.pallas_call(decode, name='decode', grid=(devices // per,), out_shape=(...  6.17 us

profile of v3, /device:TPU:1, one launch (start us, length us, event | category | flops | bytes accessed | tf_op | source)
XLA Modules:
  0.0 150.0 jit_solution(17860978050467766949)
XLA Ops:
  0.6 143.2 %step.1 = (f32[32,3072]{1,0:T(8,128)S(1)}, f32[32,3072]{1,0:T(8,128)S(1)}, f32[32,3072]{1,0:T(8,128)S(1)}, s16[32,32,3200]{2,1,0:T(8,128)(2,1)S(1)}) custom-call(s32[2,512]{1,0:T(2,128)} %bitcast.16, f32[2,512]{1,0:T(2,128)} %bitcast.17, bf16[512,3072]{1,0:T(8,128)(2,1)} %gout.1, bf16[1536,1024]{1,0:T(8,128)(2,1)} %bitcast.11, bf16[1536,1024]{1,0:T(8,128)(2,1)} %bitcast.12, ...), custom_call_target="tpu_custom_call" | custom-call | tf_op jit(solution)/shard_map/step/pallas_call | solution.py:397
  143.9 6.2 %decode.1 = (f32[1024,3072]{1,0:T(8,128)}, f32[32,3072]{1,0:T(8,128)}, f32[32,3072]{1,0:T(8,128)}, f32[32,3072]{1,0:T(8,128)}) custom-call(s16[32,32,3200]{2,1,0:T(8,128)(2,1)S(1)} %get-tuple-element.12.q_ref, f32[32,3072]{1,0:T(8,128)S(1)} %get-tuple-element.13.a_ref, f32[32,3072]{1,0:T(8,128)S(1)} %get-tuple-element.14.b_ref, ...), custom_call_target="tpu_custom_call" | custom-call | tf_op jit(solution)/shard_map/decode/pallas_call | solution.py:446

commit v4 on v3

--- a/solution.py
+++ b/solution.py
@@ -42,7 +42,7 @@
 
 
 def kernel(ids, probs, gout, gate, up, mas, mo1, mo2, nm_o, m1_o, m2_o, q_o,
-           go_v, gate_v, up_v, mas_v, m1_v, m2_v, place, wslot, H, G, acc, xacc, step_v, ssum,
+           go_v, gate_v, up_v, mas_v, m1_v, m2_v, place, wslot, H, G, acc, xacc, step_v, ssum, wrms_v,
            csend, crecv, xsend, xrecv, zsend, zrecv, own_q,
            lsem, ssem, rsem, gs, gr):
     dp = lax.axis_index("dp")
@@ -172,6 +172,8 @@
     for i in range(2, 5):
         local(C + i).wait()
     ssum[...] = jnp.zeros_like(ssum)
+    mas2 = mas_v[...] * mas_v[...]
+    wrms_v[...] = jnp.broadcast_to(jnp.sqrt(jnp.sum(mas2, axis=1, keepdims=True) / D + 1e-06), wrms_v.shape)
 
     hrows = H.shape[1]
     xrows = hrows // NX
@@ -208,7 +210,7 @@
                        pl.ds(pl.multiple_of(i * TILE, TILE), TILE))
                 return carry
 
-            lax.fori_loop(0, xrows // TILE, put, 0)
+            lax.fori_loop(0, xrows // TILE, put, 0, unroll=True)
             x_copy(c, k).start()
 
         own = pl.ds(pl.multiple_of(x * xrows, xrows), xrows)
@@ -229,7 +231,7 @@
                 xacc[c, rows, cols] = total
             return carry
 
-        lax.fori_loop(0, xrows // TILE, join, 0)
+        lax.fori_loop(0, xrows // TILE, join, 0, unroll=True)
         every = pl.ds(0, zrows)
         for k in (2, 1, 3):
             encode(xacc[c, pl.ds(pl.multiple_of(((zl + k) % NZ) * zrows, zrows), zrows), :], zsend.at[c, k - 1], every)
@@ -275,8 +277,7 @@
 
     lax.fori_loop(0, C + LAG_F, tick, 0)
 
-    mas2 = mas_v[...] * mas_v[...]
-    wrms = jnp.sqrt(jnp.sum(mas2, axis=1, keepdims=True) / D + 1e-06)
+    wrms = wrms_v[:, 0:1]
     srms = jnp.sqrt(jnp.sum(ssum[...], axis=1, keepdims=True) / D + 1e-06)
     factor = jnp.minimum(1.0, 0.02 * wrms / (0.01 * srms))
     new = mas_v[...] - 0.01 * factor * step_v[...]
@@ -420,6 +421,7 @@
             pltpu.VMEM((C, xrows, dc), f32),
             pltpu.VMEM((rows, D), f32),
             pltpu.VMEM((rows, 128), f32),
+            pltpu.VMEM((rows, 128), f32),
             pltpu.VMEM((C, hrows, dc), f32),
             pltpu.VMEM((C, hrows, dc), f32),
             pltpu.VMEM((C, NX - 1, xrows, dc + 128), i16),
@@ -441,7 +443,7 @@
         master.reshape(rows, D), moment_one.reshape(rows, D), moment_two.reshape(rows, D),
     )
     new, one, two, q = outs
-    per = 4
+    per = 8
     whole = pl.BlockSpec((rows, D), lambda i: (0, 0))
     full, new, one, two = pl.pallas_call(
         decode,

time: 151 us -> 150 us (level)
  no operation moved by 1% of the time
where the time goes in v4:
time: 150 us
  Pallas kernels  149 us (99%)
    pallas_call x1, Pallas kernels, local(): pl.pallas_call(kernel, name='step', out_shape=(pltpu.VMEM((rows, D), f32)...  143 us
    pallas_call x1, Pallas kernels, local(): pl.pallas_call(decode, name='decode', grid=(devices // per,), out_shape=(...  5.47 us

profile of v4, /device:TPU:1, one launch (start us, length us, event | category | flops | bytes accessed | tf_op | source)
XLA Modules:
  0.0 149.5 jit_solution(8783159795583987220)
XLA Ops:
  0.6 143.4 %step.1 = (f32[32,3072]{1,0:T(8,128)S(1)}, f32[32,3072]{1,0:T(8,128)S(1)}, f32[32,3072]{1,0:T(8,128)S(1)}, s16[32,32,3200]{2,1,0:T(8,128)(2,1)S(1)}) custom-call(s32[2,512]{1,0:T(2,128)} %bitcast.16, f32[2,512]{1,0:T(2,128)} %bitcast.17, bf16[512,3072]{1,0:T(8,128)(2,1)} %gout.1, bf16[1536,1024]{1,0:T(8,128)(2,1)} %bitcast.11, bf16[1536,1024]{1,0:T(8,128)(2,1)} %bitcast.12, ...), custom_call_target="tpu_custom_call" | custom-call | tf_op jit(solution)/shard_map/step/pallas_call | solution.py:398
  144.0 5.5 %decode.1 = (f32[1024,3072]{1,0:T(8,128)}, f32[32,3072]{1,0:T(8,128)}, f32[32,3072]{1,0:T(8,128)}, f32[32,3072]{1,0:T(8,128)}) custom-call(s16[32,32,3200]{2,1,0:T(8,128)(2,1)S(1)} %get-tuple-element.12.q_ref, f32[32,3072]{1,0:T(8,128)S(1)} %get-tuple-element.13.a_ref, f32[32,3072]{1,0:T(8,128)S(1)} %get-tuple-element.14.b_ref, ...), custom_call_target="tpu_custom_call" | custom-call | tf_op jit(solution)/shard_map/decode/pallas_call | solution.py:448
